TPU v7x, 128 devices: a whole 4x4x4 slice. The times are simulated.
128 devices in a mesh: row: 4 (over y_lo, core), col: 32 (over y_hi, z, x).
Axes of the slice: x: 4, y: 4 (y_hi: 2, y_lo: 2; y = y_hi * 2 + y_lo), z: 4, core: 2. Of those that a mesh axis runs over, the one named last changes fastest.
Arguments:
- sky: bfloat16 [128, 1024, 4096], P(None, 'row', 'col'), may hold values from -80 to 80
- kernel_widths: int32 [2], replicated, may hold values from 16 to 32, as said below
- prior_var: float32 [2, 128], replicated, may hold values from 0.05 to 0.5
- tile_region: int32 [4, 32], P('row', 'col'), may hold values from 0 to 7, as said below
- region_rank: int32 [8], replicated, may hold values from 2 to 8
Outputs:
- cleaned: bfloat16 [128, 1024, 4096], P(None, 'row', 'col')
Inputs may be any that keep to these rules, and one draw needn't show every extreme that they name: `kernel_widths`: entry 0 is the half-width along the sky's rows (second dimension of sky), entry 1 along its columns; one of the two equals 32, the other is below 32. `tile_region`: each region holds exactly 16 tiles, anywhere on the sky.
All inputs are finite; a program needn't handle non-finite values.
Results may differ from a plain program's by a relative error of at most 0.0085.
Values may be sent and summed in bfloat16 or wider, within the bound.
A program may use at most 128 MiB of HBM per device.

v0:
```python
import math
import jax
import jax.numpy as jnp
from jax import lax
from jax.sharding import PartitionSpec as P

HW = 32
MMAX = 8
TPR = 16


def extended_2(cells, sides, width):
    for axis, dim in sides:
        count = lax.axis_size(axis)
        ends = count - 1
        head = lax.slice_in_dim(cells, 0, width, axis=dim)
        tail = lax.slice_in_dim(cells, cells.shape[dim] - width, cells.shape[dim], axis=dim)
        cells = jnp.concatenate(
            [
                lax.ppermute(tail, axis, [(i, (i + 1) % count) for i in range(ends)]),
                cells,
                lax.ppermute(head, axis, [((i + 1) % count, i) for i in range(ends)]),
            ],
            axis=dim,
        )
    return cells


def raised(offsets, half_width):
    spread = half_width.astype(jnp.float32)
    inside = jnp.abs(offsets) <= spread
    values = (1.0 + jnp.cos(math.pi * offsets / (spread + 1.0))) / (2.0 * spread + 2.0)
    return jnp.where(inside, values, jnp.zeros_like(values))


def toeplitz(length, half_width):
    inputs = jnp.arange(length + 2 * HW, dtype=jnp.float32)[:, None]
    outputs = jnp.arange(length, dtype=jnp.float32)[None, :]
    offsets = inputs - outputs - HW
    return raised(offsets, half_width).astype(jnp.bfloat16)


def chebyshev(chan_count, degree):
    position = (2.0 * jnp.arange(chan_count, dtype=jnp.float32) + 1.0) / chan_count - 1.0
    terms = [jnp.ones_like(position), position]
    for order in range(2, degree):
        terms.append(2.0 * position * terms[-1] - terms[-2])
    return jnp.stack(terms[:degree], axis=1)


def spd_solve(matrix, right_hand):
    factor = jnp.linalg.cholesky(matrix)
    middle = lax.linalg.triangular_solve(factor, right_hand, left_side=True, lower=True)
    return lax.linalg.triangular_solve(factor, middle, left_side=True, lower=True, transpose_a=True)


def projector(gram_sum, prior_row, keep_rank, pixels):
    chan_count = gram_sum.shape[0]
    cheb_basis = chebyshev(chan_count, MMAX)
    covariance = gram_sum / pixels + jnp.diag(prior_row)
    mixed = spd_solve(covariance, cheb_basis)
    keep_mask = (jnp.arange(MMAX) < keep_rank).astype(jnp.float32)
    kept_basis = cheb_basis * keep_mask
    kept_mixed = mixed * keep_mask
    small_matrix = jnp.dot(kept_basis.T, kept_mixed, precision=lax.Precision.HIGHEST) + jnp.diag(
        1.0 - keep_mask
    )
    weights = spd_solve(small_matrix, kept_mixed.T)
    return jnp.dot(kept_basis, weights, precision=lax.Precision.HIGHEST).astype(jnp.bfloat16)


def local(sky, kernel_widths, prior_var, tile_region, region_rank):
    chan_count, tile_rows, tile_cols = sky.shape
    down_table = toeplitz(tile_rows, kernel_widths[0])
    across_table = toeplitz(tile_cols, kernel_widths[1])
    extended = extended_2(sky, (("row", 1), ("col", 2)), HW)
    smooth = jnp.einsum(
        "cyx,yz->czx", extended, down_table, preferred_element_type=jnp.float32
    ).astype(jnp.bfloat16)
    coarse = jnp.einsum(
        "cyx,xz->cyz", smooth, across_table, preferred_element_type=jnp.float32
    ).astype(jnp.bfloat16)
    fine = (sky.astype(jnp.float32) - coarse.astype(jnp.float32)).astype(jnp.bfloat16)
    coarse_gram = jnp.einsum("cyx,dyx->cd", coarse, coarse, preferred_element_type=jnp.float32)
    fine_gram = jnp.einsum("cyx,dyx->cd", fine, fine, preferred_element_type=jnp.float32)
    grams = jnp.stack([coarse_gram, fine_gram], axis=0)
    region = tile_region[0, 0]
    region_count = region_rank.shape[0]
    slot_mask = (jnp.arange(region_count) == region).astype(jnp.float32)
    slotted = slot_mask[:, None, None, None] * grams[None]
    totals = lax.psum(slotted, ("row", "col"))
    own_gram = lax.dynamic_index_in_dim(totals, region, 0, keepdims=False)
    keep_rank = lax.dynamic_index_in_dim(region_rank, region, 0, keepdims=False)
    pixels = TPR * tile_rows * tile_cols
    coarse_proj = projector(own_gram[0], prior_var[0], keep_rank, pixels)
    fine_proj = projector(own_gram[1], prior_var[1], keep_rank, pixels)
    removed = jnp.einsum("ij,jyx->iyx", coarse_proj, coarse, preferred_element_type=jnp.float32)
    removed = removed + jnp.einsum(
        "ij,jyx->iyx", fine_proj, fine, preferred_element_type=jnp.float32
    )
    cleaned = coarse.astype(jnp.float32) + fine.astype(jnp.float32) - removed
    return cleaned.astype(jnp.bfloat16)


def solution(mesh):
    return jax.shard_map(
        local,
        mesh=mesh,
        in_specs=(P(None, "row", "col"), P(), P(), P("row", "col"), P()),
        out_specs=P(None, "row", "col"),
        check_vma=False,
    )
```

profile of v0, /device:TPU:1, one launch (start us, length us, event | category | flops | bytes accessed | tf_op | source)
XLA Modules:
  0.0 505.3 jit_solution(14698396365791912761)
XLA Ops:
  6.5 12.7 %copy.25 = bf16[128,256,128]{0,2,1:T(8,128)(2,1)} copy(bf16[128,256,128]{2,1,0:T(8,128)(2,1)} %param.15) | data formatting | bytes 16777216 | tf_op args[0]
  19.2 1.7 fusion.87
  20.9 4.6 collective-permute-start
  25.5 1.9 collective-permute-start.1
  27.4 9.8 %collective-permute-done = bf16[128,32,128]{0,2,1:T(8,128)(2,1)S(1)} collective-permute-done((bf16[128,32,128]{0,2,1:T(8,128)(2,1)S(1)}, bf16[128,32,128]{0,2,1:T(8,128)(2,1)S(1)}, u32[]{:S(2)}, u32[]{:S(2)}) %collective-permute-start) | collective-permute-done | bytes 1048608 | tf_op jit(solution)/shard_map/ppermute | solution.py:20
  37.2 4.4 collective-permute-done.1
  41.6 7.7 %pad_maximum_fusion.3 = (bf16[128,320,32]{0,2,1:T(8,128)(2,1)}, bf16[128,320,32]{0,2,1:T(8,128)(2,1)}) fusion(bf16[128,32,128]{0,2,1:T(8,128)(2,1)S(1)} %collective-permute-done.1, bf16[128,256,128]{0,2,1:T(8,128)(2,1)} %copy.25, bf16[128,32,128]{0,2,1:T(8,128)(2,1)S(1)} %collective-permute-done), kind=kLoop, calls=%fused_computation.18 | loop fusion | flops 15728640 | bytes 15728640 | tf_op jit(solution)/shard_map/slice | solution.py:17
  49.3 4.6 collective-permute-start.2
  53.9 1.5 collective-permute-start.3
  55.4 0.6 fusion.88
  58.0 0.6 dynamic_slice.8
  58.7 39.6 %collective-permute-done.2 = bf16[128,320,32]{0,2,1:T(8,128)(2,1)} collective-permute-done((bf16[128,320,32]{0,2,1:T(8,128)(2,1)}, bf16[128,320,32]{0,2,1:T(8,128)(2,1)}, u32[]{:S(2)}, u32[]{:S(2)}) %collective-permute-start.2) | collective-permute-done | bytes 2621472 | tf_op jit(solution)/shard_map/ppermute | solution.py:20
  98.3 5.6 %collective-permute-done.3 = bf16[128,320,32]{0,2,1:T(8,128)(2,1)} collective-permute-done((bf16[128,320,32]{0,2,1:T(8,128)(2,1)}, bf16[128,320,32]{0,2,1:T(8,128)(2,1)}, u32[]{:S(2)}, u32[]{:S(2)}) %collective-permute-start.3) | collective-permute-done | bytes 2621472 | tf_op jit(solution)/shard_map/ppermute | solution.py:22
  103.9 29.0 %pad_maximum_fusion = bf16[128,320,192]{0,2,1:T(8,128)(2,1)} fusion(bf16[128,320,32]{0,2,1:T(8,128)(2,1)} %collective-permute-done.3, bf16[128,32,128]{0,2,1:T(8,128)(2,1)S(1)} %collective-permute-done.1, bf16[128,256,128]{0,2,1:T(8,128)(2,1)} %copy.25, bf16[128,32,128]{0,2,1:T(8,128)(2,1)S(1)} %collective-permute-done, ...), kind=kLoop, calls=%fused_computation.6 | loop fusion | flops 78643200 | bytes 31457280 | tf_op jit(solution)/shard_map/concatenate | solution.py:18
  133.0 26.4 %copy.47 = bf16[128,320,192]{1,2,0:T(8,128)(2,1)} copy(bf16[128,320,192]{0,2,1:T(8,128)(2,1)} %pad_maximum_fusion) | data formatting | bytes 31457280 | tf_op jit(solution)/shard_map/concatenate | solution.py:18
  159.3 25.8 %fusion = (bf16[128,256,128]{2,1,0:T(8,128)(2,1)}, bf16[128,256,128]{2,1,0:T(8,128)(2,1)}) fusion(bf16[128,256,128]{2,1,0:T(8,128)(2,1)} %param.15, f32[]{:T(128)S(6)} %add.184, f32[]{:T(128)S(6)} %add.181, f32[]{:T(128)} %bitcast.4, bf16[128,320,192]{1,2,0:T(8,128)(2,1)} %copy.47, f32[]{:T(128)S(6)} %add.180, f32[]{:T(128)S(6)} %add.177, f32[]{:T(128)} %bitcast.1), kind=kOutput, calls=%fused_computation.2 | convolution fusion | flops 5665472512 | bytes 40894488 | tf_op jit(solution)/shard_map/cyx,xz->cyz/dot_general | solution.py:80
  185.1 12.5 %copy.30 = bf16[128,256,128]{1,0,2:T(8,128)(2,1)} copy(bf16[128,256,128]{2,1,0:T(8,128)(2,1)} %get-tuple-element.21) | data formatting | bytes 16777216 | tf_op jit(solution)/shard_map/convert_element_type | solution.py:83
  197.7 8.1 %convolution_bitcast_fusion = f32[1,128,128]{2,1,0:T(8,128)S(1)} fusion(bf16[128,256,128]{1,0,2:T(8,128)(2,1)} %copy.30), kind=kOutput, calls=%fused_computation.19 | convolution fusion | flops 1073741824 | bytes 8454144 | tf_op jit(solution)/shard_map/cyx,dyx->cd/dot_general | solution.py:85
  205.8 12.9 %copy.28 = bf16[128,256,128]{1,0,2:T(8,128)(2,1)} copy(bf16[128,256,128]{2,1,0:T(8,128)(2,1)} %get-tuple-element.22) | data formatting | bytes 16777216 | tf_op jit(solution)/shard_map/convert_element_type | solution.py:82
  218.7 8.1 %convolution_bitcast_fusion.1 = f32[1,128,128]{2,1,0:T(8,128)S(1)} fusion(bf16[128,256,128]{1,0,2:T(8,128)(2,1)} %copy.28), kind=kOutput, calls=%fused_computation.20 | convolution fusion | flops 1073741824 | bytes 8454144 | tf_op jit(solution)/shard_map/cyx,dyx->cd/dot_general | solution.py:84
  226.9 1.2 broadcast_multiply_fusion
  228.2 0.6 compare_convert_fusion.1
  228.8 0.6 broadcast_subtract_fusion
  229.5 150.2 %all-reduce.2.cloned.1.call-done = f32[8,2,128,128]{2,3,1,0:T(8,128)} async-done(((f32[8,2,128,128]{2,3,1,0:T(8,128)}), f32[8,2,128,128]{2,3,1,0:T(8,128)}) %all-reduce.2.cloned.1.call-update) | async-done | bytes 1048592 | tf_op jit(solution)/shard_map/psum | solution.py:91
  379.7 0.9 fusion.39
  380.9 11.7 %cholesky.108 = f32[128,128]{1,0:T(8,128)S(1)} custom-call(f32[128,128]{1,0:T(8,128)S(1)} %get-tuple-element.29), custom_call_target="Cholesky" | custom-call | tf_op jit(solution)/shard_map/jit(cholesky)/cholesky | solution.py:52
  392.6 0.7 compare_reduce_fusion.1
  393.3 0.6 fusion.35
  393.9 9.8 %custom-call.25 = f32[1,128,128]{1,2,0:T(8,128)S(1)} custom-call(f32[1,128,128]{2,1,0:T(8,128)S(1)} %fusion.35), custom_call_target="InvertDiagBlocksLowerTriangular" | custom-call | tf_op jit(solution)/shard_map/triangular_solve/custom-call.3 | solution.py:54
  403.7 11.7 %cholesky.86 = f32[128,128]{1,0:T(8,128)S(1)} custom-call(f32[128,128]{1,0:T(8,128)S(1)} %get-tuple-element.30), custom_call_target="Cholesky" | custom-call | tf_op jit(solution)/shard_map/jit(cholesky)/cholesky | solution.py:52
  415.5 0.7 compare_reduce_fusion.3
  416.2 0.6 fusion.34
  416.8 10.0 %custom-call.21 = f32[1,128,128]{1,2,0:T(8,128)S(1)} custom-call(f32[1,128,128]{2,1,0:T(8,128)S(1)} %fusion.34), custom_call_target="InvertDiagBlocksLowerTriangular" | custom-call | tf_op jit(solution)/shard_map/triangular_solve/custom-call.3 | solution.py:54
  426.8 0.3 fusion.44
  427.6 0.7 cholesky.97
  428.4 0.7 compare_reduce_fusion.2
  429.0 0.6 fusion.57
  429.7 0.6 custom-call.23
  430.6 0.4 fusion.15
  431.0 0.3 fusion.40
  431.8 0.7 cholesky.119
  432.6 0.7 compare_reduce_fusion
  433.3 0.6 fusion.58
  433.9 0.6 custom-call.27
  434.9 0.4 fusion.16
  435.3 15.6 %fusion.8 = f32[128,256,128]{2,0,1:T(8,128)} fusion(bf16[128,128,1]{1,0,2:T(8,128)(2,1)S(1)} %fusion.16, bf16[128,256,128]{2,1,0:T(8,128)(2,1)} %get-tuple-element.21), kind=kOutput, calls=%fused_computation.11 | convolution fusion | flops 1073741824 | bytes 25198592 | tf_op jit(solution)/shard_map/ij,jyx->iyx/dot_general | solution.py:98
  450.8 15.8 %fusion.10 = f32[128,256,128]{2,0,1:T(8,128)} fusion(bf16[128,128,1]{1,0,2:T(8,128)(2,1)S(1)} %fusion.15, bf16[128,256,128]{2,1,0:T(8,128)(2,1)} %get-tuple-element.22), kind=kOutput, calls=%fused_computation.13 | convolution fusion | flops 1073741824 | bytes 25198592 | tf_op jit(solution)/shard_map/ij,jyx->iyx/dot_general | solution.py:97
  466.6 31.6 %fusion.2 = bf16[128,256,128]{2,1,0:T(8,128)(2,1)} fusion(bf16[128,256,128]{2,1,0:T(8,128)(2,1)S(1)} %bitcast.129, f32[128,256,128]{2,0,1:T(8,128)} %fusion.8, f32[128,256,128]{2,0,1:T(8,128)} %fusion.10, bf16[128,256,128]{2,1,0:T(8,128)(2,1)S(1)} %bitcast.131), kind=kLoop, calls=%fused_computation.4 | loop fusion | flops 37748736 | bytes 58720256 | tf_op jit(solution)/shard_map/convert_element_type | solution.py:102
  (47 shorter events, 2.4 us)
Async XLA Ops:
  6.5 373.2 %all-reduce.2.cloned.1.call-start = ((), (), s32[]{:S(2)}) async-start(), calls=%async_computation | async-start | bytes 2097152 | tf_op jit(solution)/shard_map/psum | solution.py:91
  20.9 34.5 %copy-start = (s32[2]{0:T(128)S(1)}, s32[2]{0:T(128)}, u32[]{:S(2)}) copy-start(s32[2]{0:T(128)} %param.16) | copy-start | bytes 28
  20.9 37.1 %copy-start.2 = (s32[8]{0:T(128)S(1)}, s32[8]{0:T(128)}, u32[]{:S(2)}) copy-start(s32[8]{0:T(128)} %param.19) | copy-start | bytes 100
  20.9 16.3 %collective-permute-start = (bf16[128,32,128]{0,2,1:T(8,128)(2,1)S(1)}, bf16[128,32,128]{0,2,1:T(8,128)(2,1)S(1)}, u32[]{:S(2)}, u32[]{:S(2)}) collective-permute-start(bf16[128,32,128]{0,2,1:T(8,128)(2,1)S(1)} %get-tuple-element.10), channel_id=1, source_target_pairs={{0,32},{32,64},{64,96},{1,33},{33,65},{65,97},{2,34},{34,66},{66,9... | collective-permute-start | bytes 3145736 | tf_op jit(solution)/shard_map/ppermute | solution.py:20
  25.5 16.1 %collective-permute-start.1 = (bf16[128,32,128]{0,2,1:T(8,128)(2,1)S(1)}, bf16[128,32,128]{0,2,1:T(8,128)(2,1)S(1)}, u32[]{:S(2)}, u32[]{:S(2)}) collective-permute-start(bf16[128,32,128]{0,2,1:T(8,128)(2,1)S(1)} %get-tuple-element.12), channel_id=1, source_target_pairs={{32,0},{64,32},{96,64},{33,1},{65,33},{97,65},{34,2},{66,34},{98,6... | collective-permute-start | bytes 3145736 | tf_op jit(solution)/shard_map/ppermute | solution.py:22
  49.3 49.0 %collective-permute-start.2 = (bf16[128,320,32]{0,2,1:T(8,128)(2,1)}, bf16[128,320,32]{0,2,1:T(8,128)(2,1)}, u32[]{:S(2)}, u32[]{:S(2)}) collective-permute-start(bf16[128,320,32]{0,2,1:T(8,128)(2,1)} %get-tuple-element.6), channel_id=1, source_target_pairs={{0,1},{1,2},{2,3},{3,4},{4,5},{5,6},{6,7},{7,8},{8,9},{9,10},{10,1... | collective-permute-start | bytes 7864328 | tf_op jit(solution)/shard_map/ppermute | solution.py:20
  53.9 50.0 %collective-permute-start.3 = (bf16[128,320,32]{0,2,1:T(8,128)(2,1)}, bf16[128,320,32]{0,2,1:T(8,128)(2,1)}, u32[]{:S(2)}, u32[]{:S(2)}) collective-permute-start(bf16[128,320,32]{0,2,1:T(8,128)(2,1)} %get-tuple-element.8), channel_id=1, source_target_pairs={{1,0},{2,1},{3,2},{4,3},{5,4},{6,5},{7,6},{8,7},{9,8},{10,9},{11,1... | collective-permute-start | bytes 7864328 | tf_op jit(solution)/shard_map/ppermute | solution.py:22
  218.7 10.8 %copy-start.1 = (f32[2,128]{1,0:T(2,128)S(1)}, f32[2,128]{1,0:T(2,128)}, u32[]{:S(2)}) copy-start(f32[2,128]{1,0:T(2,128)} %param.17) | copy-start | bytes 3076
  435.2 31.4 %slice-start = ((s8[8388608]{0:T(1024)(128)(4,1)}), s8[4194304]{0:T(1024)(128)(4,1)S(1)}, s32[]{:S(2)}) async-start(s8[8388608]{0:T(1024)(128)(4,1)} %bitcast.128), calls=%async_computation.1 | async-start | bytes 8388608
  435.2 31.4 %slice-start.2 = ((s8[8388608]{0:T(1024)(128)(4,1)}), s8[4194304]{0:T(1024)(128)(4,1)S(1)}, s32[]{:S(2)}) async-start(s8[8388608]{0:T(1024)(128)(4,1)} %bitcast.130), calls=%async_computation.3 | async-start | bytes 8388608
  450.8 15.8 %slice-start.1 = ((s8[8388608]{0:T(1024)(128)(4,1)}), s8[4194304]{0:T(1024)(128)(4,1)S(1)}, s32[]{:S(2)}) async-start(s8[8388608]{0:T(1024)(128)(4,1)} %bitcast.128), calls=%async_computation.2 | async-start | bytes 8388608
  450.8 15.8 %slice-start.3 = ((s8[8388608]{0:T(1024)(128)(4,1)}), s8[4194304]{0:T(1024)(128)(4,1)S(1)}, s32[]{:S(2)}) async-start(s8[8388608]{0:T(1024)(128)(4,1)} %bitcast.130), calls=%async_computation.4 | async-start | bytes 8388608
Sparse Core Ops, SparseCore 0:
  228.3 151.4 all-reduce.1
where the time goes:
time: 510 us; the launch traced here: 505 us
  waiting for transfers between devices  210 us (41%)
  other arithmetic  123 us (24%)
  matrix products  76.2 us (15%)
  local copies, waits for them, and re-layouts  68 us (13%)
  between operations  15.9 us (3%)
  starting transfers between devices  12.6 us (2%)
    psum x1, waiting for transfers between devices, local(): totals = lax.psum(slotted, ('row', 'col'))  150 us
    ppermute x2, waiting for transfers between devices, extended_2(): lax.ppermute(tail, axis, [(i, (i + 1) % count) for i in range(ends)])  49.4 us
    convert_element_type x1, other arithmetic, local(): return cleaned.astype(jnp.bfloat16)  31.6 us
    concatenate x1, other arithmetic, extended_2(): jnp.concatenate([lax.ppermute(tail, axis, [(i, (i + 1) % count) for i in...  29 us
    another operation x12, other arithmetic, spd_solve(): factor = jnp.linalg.cholesky(matrix)  27.7 us
    concatenate x1, local copies, waits for them, and re-layouts, extended_2(): jnp.concatenate([lax.ppermute(tail, axis, [(i, (i + 1) % count) for i in...  26.4 us
    dot_general x1, matrix products, local(): jnp.einsum('cyx,xz->cyz', smooth, across_table, preferred_element_type=jn...  25.8 us
    another operation x8, other arithmetic, spd_solve(): lax.linalg.triangular_solve(factor, middle, left_side=True, lower=True, t...  23.6 us
  transfers between devices with their start and end apart: 5, of which 5 were waited for; matrix products, arithmetic and copies ran while one was open for 1% of the time, Pallas kernels for 0%

commit v1 on v0

--- a/solution.py
+++ b/solution.py
@@ -88,7 +88,9 @@
     region_count = region_rank.shape[0]
     slot_mask = (jnp.arange(region_count) == region).astype(jnp.float32)
     slotted = slot_mask[:, None, None, None] * grams[None]
-    totals = lax.psum(slotted, ("row", "col"))
+    totals = slotted
+    for mesh_axis in ("col", "row"):
+        totals = lax.psum(totals, mesh_axis)
     own_gram = lax.dynamic_index_in_dim(totals, region, 0, keepdims=False)
     keep_rank = lax.dynamic_index_in_dim(region_rank, region, 0, keepdims=False)
     pixels = TPR * tile_rows * tile_cols

time: 510 us -> 761 us (1.49)
  waiting for transfers between devices: 210 us -> 460 us
    psum x1 -> x2, waiting for transfers between devices: 150 us -> 401 us  [local(): totals = lax.psum(totals, mesh_axis)]
  transfers between devices with their start and end apart: 5 -> 6, of which waited for: 5 -> 6; matrix products, arithmetic and copies ran while one was open for 1% -> 0% of each run, Pallas kernels for 0% -> 0%
where the time goes in v1:
time: 761 us; the launch traced here: 756 us
  waiting for transfers between devices  460 us (60%)
  other arithmetic  123 us (16%)
  matrix products  76.2 us (10%)
  local copies, waits for them, and re-layouts  67.7 us (9%)
  between operations  16.1 us (2%)
  starting transfers between devices  13 us (2%)
    psum x2, waiting for transfers between devices, local(): totals = lax.psum(totals, mesh_axis)  401 us
    ppermute x2, waiting for transfers between devices, extended_2(): lax.ppermute(tail, axis, [(i, (i + 1) % count) for i in range(ends)])  49.7 us
    convert_element_type x1, other arithmetic, local(): return cleaned.astype(jnp.bfloat16)  31.6 us
    concatenate x1, other arithmetic, extended_2(): jnp.concatenate([lax.ppermute(tail, axis, [(i, (i + 1) % count) for i in...  29 us
    another operation x12, other arithmetic, spd_solve(): factor = jnp.linalg.cholesky(matrix)  27.7 us
    concatenate x1, local copies, waits for them, and re-layouts, extended_2(): jnp.concatenate([lax.ppermute(tail, axis, [(i, (i + 1) % count) for i in...  26.4 us
    dot_general x1, matrix products, local(): jnp.einsum('cyx,xz->cyz', smooth, across_table, preferred_element_type=jn...  25.8 us
    another operation x8, other arithmetic, spd_solve(): lax.linalg.triangular_solve(factor, middle, left_side=True, lower=True, t...  23.6 us
  transfers between devices with their start and end apart: 6, of which 6 were waited for; matrix products, arithmetic and copies ran while one was open for 0% of the time, Pallas kernels for 0%

profile of v1, /device:TPU:1, one launch (start us, length us, event | category | flops | bytes accessed | tf_op | source)
XLA Modules:
  0.0 756.5 jit_solution(10722234215328519609)
XLA Ops:
  6.5 12.7 %copy.25 = bf16[128,256,128]{0,2,1:T(8,128)(2,1)} copy(bf16[128,256,128]{2,1,0:T(8,128)(2,1)} %param.15) | data formatting | bytes 16777216 | tf_op args[0]
  19.2 1.7 fusion.87
  20.9 4.6 collective-permute-start
  25.5 1.9 collective-permute-start.1
  27.4 9.8 %collective-permute-done = bf16[128,32,128]{0,2,1:T(8,128)(2,1)S(1)} collective-permute-done((bf16[128,32,128]{0,2,1:T(8,128)(2,1)S(1)}, bf16[128,32,128]{0,2,1:T(8,128)(2,1)S(1)}, u32[]{:S(2)}, u32[]{:S(2)}) %collective-permute-start) | collective-permute-done | bytes 1048608 | tf_op jit(solution)/shard_map/ppermute | solution.py:20
  37.2 4.4 collective-permute-done.1
  41.6 7.7 %pad_maximum_fusion.3 = (bf16[128,320,32]{0,2,1:T(8,128)(2,1)}, bf16[128,320,32]{0,2,1:T(8,128)(2,1)}) fusion(bf16[128,32,128]{0,2,1:T(8,128)(2,1)S(1)} %collective-permute-done.1, bf16[128,256,128]{0,2,1:T(8,128)(2,1)} %copy.25, bf16[128,32,128]{0,2,1:T(8,128)(2,1)S(1)} %collective-permute-done), kind=kLoop, calls=%fused_computation.18 | loop fusion | flops 15728640 | bytes 15728640 | tf_op jit(solution)/shard_map/slice | solution.py:17
  49.3 4.6 collective-permute-start.2
  53.9 1.8 collective-permute-start.3
  55.8 0.6 fusion.88
  58.4 40.0 %collective-permute-done.2 = bf16[128,320,32]{0,2,1:T(8,128)(2,1)} collective-permute-done((bf16[128,320,32]{0,2,1:T(8,128)(2,1)}, bf16[128,320,32]{0,2,1:T(8,128)(2,1)}, u32[]{:S(2)}, u32[]{:S(2)}) %collective-permute-start.2) | collective-permute-done | bytes 2621472 | tf_op jit(solution)/shard_map/ppermute | solution.py:20
  98.3 5.6 collective-permute-done.3
  103.9 29.0 %pad_maximum_fusion = bf16[128,320,192]{0,2,1:T(8,128)(2,1)} fusion(bf16[128,320,32]{0,2,1:T(8,128)(2,1)} %collective-permute-done.3, bf16[128,32,128]{0,2,1:T(8,128)(2,1)S(1)} %collective-permute-done.1, bf16[128,256,128]{0,2,1:T(8,128)(2,1)} %copy.25, bf16[128,32,128]{0,2,1:T(8,128)(2,1)S(1)} %collective-permute-done, ...), kind=kLoop, calls=%fused_computation.6 | loop fusion | flops 78643200 | bytes 31457280 | tf_op jit(solution)/shard_map/concatenate | solution.py:18
  132.9 26.4 %copy.47 = bf16[128,320,192]{1,2,0:T(8,128)(2,1)} copy(bf16[128,320,192]{0,2,1:T(8,128)(2,1)} %pad_maximum_fusion) | data formatting | bytes 31457280 | tf_op jit(solution)/shard_map/concatenate | solution.py:18
  159.3 25.8 %fusion = (bf16[128,256,128]{2,1,0:T(8,128)(2,1)}, bf16[128,256,128]{2,1,0:T(8,128)(2,1)}) fusion(bf16[128,256,128]{2,1,0:T(8,128)(2,1)} %param.15, f32[]{:T(128)S(6)} %add.186, f32[]{:T(128)S(6)} %add.183, f32[]{:T(128)} %bitcast.4, bf16[128,320,192]{1,2,0:T(8,128)(2,1)} %copy.47, f32[]{:T(128)S(6)} %add.182, f32[]{:T(128)S(6)} %add.179, f32[]{:T(128)} %bitcast.1), kind=kOutput, calls=%fused_computation.2 | convolution fusion | flops 5665472512 | bytes 40894488 | tf_op jit(solution)/shard_map/cyx,xz->cyz/dot_general | solution.py:80
  185.1 12.7 %copy.30 = bf16[128,256,128]{1,0,2:T(8,128)(2,1)} copy(bf16[128,256,128]{2,1,0:T(8,128)(2,1)} %get-tuple-element.21) | data formatting | bytes 16777216 | tf_op jit(solution)/shard_map/convert_element_type | solution.py:83
  197.8 8.1 %convolution_bitcast_fusion = f32[1,128,128]{2,1,0:T(8,128)S(1)} fusion(bf16[128,256,128]{1,0,2:T(8,128)(2,1)} %copy.30), kind=kOutput, calls=%fused_computation.19 | convolution fusion | flops 1073741824 | bytes 8454144 | tf_op jit(solution)/shard_map/cyx,dyx->cd/dot_general | solution.py:85
  205.9 12.6 %copy.28 = bf16[128,256,128]{1,0,2:T(8,128)(2,1)} copy(bf16[128,256,128]{2,1,0:T(8,128)(2,1)} %get-tuple-element.22) | data formatting | bytes 16777216 | tf_op jit(solution)/shard_map/convert_element_type | solution.py:82
  218.5 8.1 %convolution_bitcast_fusion.1 = f32[1,128,128]{2,1,0:T(8,128)S(1)} fusion(bf16[128,256,128]{1,0,2:T(8,128)(2,1)} %copy.28), kind=kOutput, calls=%fused_computation.20 | convolution fusion | flops 1073741824 | bytes 8454144 | tf_op jit(solution)/shard_map/cyx,dyx->cd/dot_general | solution.py:84
  226.7 1.2 broadcast_multiply_fusion
  228.0 337.1 %all-reduce.3.cloned.1.call-done = f32[8,2,128,128]{2,3,1,0:T(8,128)} async-done(((f32[8,2,128,128]{2,3,1,0:T(8,128)}), f32[8,2,128,128]{2,3,1,0:T(8,128)}) %all-reduce.3.cloned.1.call-update) | async-done | bytes 1048592 | tf_op jit(solution)/shard_map/psum | solution.py:93
  565.1 0.6 dynamic_slice.8
  565.8 0.6 compare_convert_fusion.1
  566.5 0.6 broadcast_subtract_fusion
  567.1 63.5 %all-reduce.5.cloned.1.call-done = f32[8,2,128,128]{2,3,1,0:T(8,128)} async-done(((f32[8,2,128,128]{2,3,1,0:T(8,128)}), f32[8,2,128,128]{2,3,1,0:T(8,128)}) %all-reduce.5.cloned.1.call-update) | async-done | bytes 1048592 | tf_op jit(solution)/shard_map/psum | solution.py:93
  630.6 0.9 fusion.39
  631.8 11.7 %cholesky.108 = f32[128,128]{1,0:T(8,128)S(1)} custom-call(f32[128,128]{1,0:T(8,128)S(1)} %get-tuple-element.29), custom_call_target="Cholesky" | custom-call | tf_op jit(solution)/shard_map/jit(cholesky)/cholesky | solution.py:52
  643.5 0.7 compare_reduce_fusion.1
  644.2 0.6 fusion.35
  644.8 9.8 %custom-call.25 = f32[1,128,128]{1,2,0:T(8,128)S(1)} custom-call(f32[1,128,128]{2,1,0:T(8,128)S(1)} %fusion.35), custom_call_target="InvertDiagBlocksLowerTriangular" | custom-call | tf_op jit(solution)/shard_map/triangular_solve/custom-call.3 | solution.py:54
  654.6 11.7 %cholesky.86 = f32[128,128]{1,0:T(8,128)S(1)} custom-call(f32[128,128]{1,0:T(8,128)S(1)} %get-tuple-element.30), custom_call_target="Cholesky" | custom-call | tf_op jit(solution)/shard_map/jit(cholesky)/cholesky | solution.py:52
  666.4 0.7 compare_reduce_fusion.3
  667.1 0.6 fusion.34
  667.7 10.0 %custom-call.21 = f32[1,128,128]{1,2,0:T(8,128)S(1)} custom-call(f32[1,128,128]{2,1,0:T(8,128)S(1)} %fusion.34), custom_call_target="InvertDiagBlocksLowerTriangular" | custom-call | tf_op jit(solution)/shard_map/triangular_solve/custom-call.3 | solution.py:54
  678.5 0.7 cholesky.97
  679.3 0.7 compare_reduce_fusion.2
  680.0 0.6 fusion.57
  680.6 0.6 custom-call.23
  681.6 0.4 fusion.15
  681.9 0.3 fusion.40
  682.8 0.7 cholesky.119
  683.5 0.7 compare_reduce_fusion
  684.2 0.6 fusion.58
  684.8 0.6 custom-call.27
  685.8 0.4 fusion.16
  686.2 15.6 %fusion.8 = f32[128,256,128]{2,0,1:T(8,128)} fusion(bf16[128,128,1]{1,0,2:T(8,128)(2,1)S(1)} %fusion.16, bf16[128,256,128]{2,1,0:T(8,128)(2,1)} %get-tuple-element.21), kind=kOutput, calls=%fused_computation.11 | convolution fusion | flops 1073741824 | bytes 25198592 | tf_op jit(solution)/shard_map/ij,jyx->iyx/dot_general | solution.py:100
  701.8 15.8 %fusion.10 = f32[128,256,128]{2,0,1:T(8,128)} fusion(bf16[128,128,1]{1,0,2:T(8,128)(2,1)S(1)} %fusion.15, bf16[128,256,128]{2,1,0:T(8,128)(2,1)} %get-tuple-element.22), kind=kOutput, calls=%fused_computation.13 | convolution fusion | flops 1073741824 | bytes 25198592 | tf_op jit(solution)/shard_map/ij,jyx->iyx/dot_general | solution.py:99
  717.6 31.6 %fusion.2 = bf16[128,256,128]{2,1,0:T(8,128)(2,1)} fusion(bf16[128,256,128]{2,1,0:T(8,128)(2,1)S(1)} %bitcast.129, f32[128,256,128]{2,0,1:T(8,128)} %fusion.8, f32[128,256,128]{2,0,1:T(8,128)} %fusion.10, bf16[128,256,128]{2,1,0:T(8,128)(2,1)S(1)} %bitcast.131), kind=kLoop, calls=%fused_computation.4 | loop fusion | flops 37748736 | bytes 58720256 | tf_op jit(solution)/shard_map/convert_element_type | solution.py:104
  (50 shorter events, 2.7 us)
Async XLA Ops:
  6.5 558.6 %all-reduce.3.cloned.1.call-start = ((), (), s32[]{:S(2)}) async-start(), calls=%async_computation | async-start | bytes 2097152 | tf_op jit(solution)/shard_map/psum | solution.py:93
  20.9 34.9 %copy-start = (s32[2]{0:T(128)S(1)}, s32[2]{0:T(128)}, u32[]{:S(2)}) copy-start(s32[2]{0:T(128)} %param.16) | copy-start | bytes 28
  20.9 16.3 %collective-permute-start = (bf16[128,32,128]{0,2,1:T(8,128)(2,1)S(1)}, bf16[128,32,128]{0,2,1:T(8,128)(2,1)S(1)}, u32[]{:S(2)}, u32[]{:S(2)}) collective-permute-start(bf16[128,32,128]{0,2,1:T(8,128)(2,1)S(1)} %get-tuple-element.10), channel_id=1, source_target_pairs={{0,32},{32,64},{64,96},{1,33},{33,65},{65,97},{2,34},{34,66},{66,9... | collective-permute-start | bytes 3145736 | tf_op jit(solution)/shard_map/ppermute | solution.py:20
  25.5 16.1 %collective-permute-start.1 = (bf16[128,32,128]{0,2,1:T(8,128)(2,1)S(1)}, bf16[128,32,128]{0,2,1:T(8,128)(2,1)S(1)}, u32[]{:S(2)}, u32[]{:S(2)}) collective-permute-start(bf16[128,32,128]{0,2,1:T(8,128)(2,1)S(1)} %get-tuple-element.12), channel_id=1, source_target_pairs={{32,0},{64,32},{96,64},{33,1},{65,33},{97,65},{34,2},{66,34},{98,6... | collective-permute-start | bytes 3145736 | tf_op jit(solution)/shard_map/ppermute | solution.py:22
  49.3 49.0 %collective-permute-start.2 = (bf16[128,320,32]{0,2,1:T(8,128)(2,1)}, bf16[128,320,32]{0,2,1:T(8,128)(2,1)}, u32[]{:S(2)}, u32[]{:S(2)}) collective-permute-start(bf16[128,320,32]{0,2,1:T(8,128)(2,1)} %get-tuple-element.6), channel_id=1, source_target_pairs={{0,1},{1,2},{2,3},{3,4},{4,5},{5,6},{6,7},{7,8},{8,9},{9,10},{10,1... | collective-permute-start | bytes 7864328 | tf_op jit(solution)/shard_map/ppermute | solution.py:20
  53.9 50.0 %collective-permute-start.3 = (bf16[128,320,32]{0,2,1:T(8,128)(2,1)}, bf16[128,320,32]{0,2,1:T(8,128)(2,1)}, u32[]{:S(2)}, u32[]{:S(2)}) collective-permute-start(bf16[128,320,32]{0,2,1:T(8,128)(2,1)} %get-tuple-element.8), channel_id=1, source_target_pairs={{1,0},{2,1},{3,2},{4,3},{5,4},{6,5},{7,6},{8,7},{9,8},{10,9},{11,1... | collective-permute-start | bytes 7864328 | tf_op jit(solution)/shard_map/ppermute | solution.py:22
  218.5 346.7 %copy-start.2 = (s32[8]{0:T(128)S(1)}, s32[8]{0:T(128)}, u32[]{:S(2)}) copy-start(s32[8]{0:T(128)} %param.19) | copy-start | bytes 100
  218.5 348.6 %copy-start.1 = (f32[2,128]{1,0:T(2,128)S(1)}, f32[2,128]{1,0:T(2,128)}, u32[]{:S(2)}) copy-start(f32[2,128]{1,0:T(2,128)} %param.17) | copy-start | bytes 3076
  227.9 402.7 %all-reduce.5.cloned.1.call-start = ((), (), s32[]{:S(2)}) async-start(), calls=%async_computation.1 | async-start | bytes 2097152 | tf_op jit(solution)/shard_map/psum | solution.py:93
  686.2 31.4 %slice-start = ((s8[8388608]{0:T(1024)(128)(4,1)}), s8[4194304]{0:T(1024)(128)(4,1)S(1)}, s32[]{:S(2)}) async-start(s8[8388608]{0:T(1024)(128)(4,1)} %bitcast.128), calls=%async_computation.2 | async-start | bytes 8388608
  686.2 31.4 %slice-start.2 = ((s8[8388608]{0:T(1024)(128)(4,1)}), s8[4194304]{0:T(1024)(128)(4,1)S(1)}, s32[]{:S(2)}) async-start(s8[8388608]{0:T(1024)(128)(4,1)} %bitcast.130), calls=%async_computation.4 | async-start | bytes 8388608
  701.8 15.8 %slice-start.1 = ((s8[8388608]{0:T(1024)(128)(4,1)}), s8[4194304]{0:T(1024)(128)(4,1)S(1)}, s32[]{:S(2)}) async-start(s8[8388608]{0:T(1024)(128)(4,1)} %bitcast.128), calls=%async_computation.3 | async-start | bytes 8388608
  701.8 15.8 %slice-start.3 = ((s8[8388608]{0:T(1024)(128)(4,1)}), s8[4194304]{0:T(1024)(128)(4,1)S(1)}, s32[]{:S(2)}) async-start(s8[8388608]{0:T(1024)(128)(4,1)} %bitcast.130), calls=%async_computation.5 | async-start | bytes 8388608
Sparse Core Ops, SparseCore 0:
  228.0 336.9 all-reduce.2
  567.6 62.9 all-reduce.4
